TPU v7x, 32 devices: a whole 2x2x4 slice. The times are simulated.
32 devices in a mesh: dp: 4 (over z), tensor: 8 (over y, x, core).
Axes of the slice: x: 2, y: 2, z: 4, core: 2. Of those that a mesh axis runs over, the one named last changes fastest.
Arguments:
- tokens: bfloat16 [8192, 1152], P('dp'), may hold values from -6 to 6
- condition: float32 [32, 1152], P('dp'), may hold values from -6 to 6
- timesteps: int32 [32], P('dp'), may hold values from 0 to 999
- route_masks: int32 [1000, 16, 2], P(None, 'tensor'), may hold values 0 or 1
- modulate_weight: bfloat16 [1152, 6, 1152], P(None, None, 'tensor'), may hold values from -0.1875 to 0.1875
- modulate_bias: bfloat16 [6, 1152], P(None, 'tensor'), may hold values from -1.5 to 1.5
- input_weight: bfloat16 [1152, 3, 1152], P(None, None, 'tensor'), may hold values from -0.1875 to 0.1875
- input_bias: bfloat16 [2, 1152], P(None, 'tensor'), may hold values from -1.5 to 1.5
- output_weight: bfloat16 [1152, 1152], P('tensor'), may hold values from -1.5 to 1.5
- output_bias: bfloat16 [1152], replicated, may hold values from -1.5 to 1.5
- expand_weight: bfloat16 [1152, 4608], P(None, 'tensor'), may hold values from -0.1875 to 0.1875
- expand_bias: bfloat16 [4608], P('tensor'), may hold values from -1.5 to 1.5
- reduce_weight: bfloat16 [4608, 1152], P('tensor'), may hold values from -0.1875 to 0.1875
- reduce_bias: bfloat16 [1152], replicated, may hold values from -1.5 to 1.5
- router_weight: bfloat16 [1152, 16, 2], P(None, 'tensor'), may hold values from -0.1875 to 0.1875
- router_bias: bfloat16 [16, 2], P('tensor'), may hold values from -1.2 to 1.2
- out_cotangent: bfloat16 [8192, 1152], P('dp'), may hold values from -6 to 6
Outputs:
- block_output: float32 [8192, 1152], P('dp')
- tokens_grad: float32 [8192, 1152], P('dp')
- modulate_weight_grad: float32 [1152, 6, 1152], P(None, None, 'tensor')
- modulate_bias_grad: float32 [6, 1152], P(None, 'tensor')
- input_weight_grad: float32 [1152, 3, 1152], P(None, None, 'tensor')
- input_bias_grad: float32 [2, 1152], P(None, 'tensor')
- output_weight_grad: float32 [1152, 1152], P('tensor')
- output_bias_grad: float32 [1152], replicated
- expand_weight_grad: float32 [1152, 4608], P(None, 'tensor')
- expand_bias_grad: float32 [4608], P('tensor')
- reduce_weight_grad: float32 [4608, 1152], P('tensor')
- reduce_bias_grad: float32 [1152], replicated
- router_weight_grad: float32 [1152, 16, 2], P(None, 'tensor')
- router_bias_grad: float32 [16, 2], P('tensor')
Inputs may be any that keep to these rules, and one draw needn't show every extreme that they name: `timesteps`: each timestep selects the row of route_masks used by its item.
All inputs are finite; a program needn't handle non-finite values. No bound on the sum of `route_masks` on one device may be relied on, other than what follows from the above.
Results may differ from a plain program's by a relative error of at most 0.013.
The roundings to bfloat16 on the way count: a program that leaves them out, or rounds other values in their place, can miss the bound.
Values may be sent and summed in bfloat16 or wider, within the bound.
A program may use at most 256 MiB of HBM per device.

v0:
```python
import math
import jax
import jax.numpy as jnp
from jax import lax
from jax.sharding import PartitionSpec as P

HIGHEST = lax.Precision.HIGHEST
EPSILON = 1e-06


def layer_norm(values):
    center = values - jnp.mean(values, axis=-1, keepdims=True)
    inverse = lax.rsqrt(jnp.mean(center * center, axis=-1, keepdims=True) + EPSILON)
    return (center * inverse, inverse)


def norm_back(grad_norm, normed, inverse):
    mean_grad = jnp.mean(grad_norm, axis=-1, keepdims=True)
    mean_cross = jnp.mean(grad_norm * normed, axis=-1, keepdims=True)
    return inverse * (grad_norm - mean_grad - normed * mean_cross)


def gelu_tanh(values):
    return jax.nn.gelu(values, approximate=True)


def contract_rows(left, right):
    return lax.dot_general(
        left, right, (((0,), (0,)), ((), ())), preferred_element_type=jnp.float32
    )


def contract_cols(left, right):
    return lax.dot_general(
        left, right, (((1,), (1,)), ((), ())), preferred_element_type=jnp.float32
    )


def body(
    tokens,
    condition,
    timesteps,
    route_masks,
    modulate_weight,
    modulate_bias,
    input_weight,
    input_bias,
    output_weight,
    output_bias,
    expand_weight,
    expand_bias,
    reduce_weight,
    reduce_bias,
    router_weight,
    router_bias,
    out_cotangent,
):
    model_width = tokens.shape[1]
    item_count = condition.shape[0]
    rows_all = tokens.shape[0]
    item_length = rows_all // item_count
    local_heads = router_weight.shape[1]
    local_width = input_weight.shape[2]
    head_size = local_width // local_heads
    group_width = expand_weight.shape[1] // local_heads
    score_scale = 1.0 / math.sqrt(head_size)
    silu_condition = jax.nn.silu(condition).astype(jnp.bfloat16)
    condition_low = condition.astype(jnp.bfloat16)
    modulate_part = jnp.einsum(
        "bd,dke->bke", silu_condition, modulate_weight, preferred_element_type=jnp.float32
    ) + modulate_bias.astype(jnp.float32)
    modulation = lax.all_gather(modulate_part, "tensor", axis=2, tiled=True)
    shift_one, scale_one, gate_one, shift_two, scale_two, gate_two = [
        modulation[:, column][:, None, :] for column in range(6)
    ]
    logits = jnp.einsum(
        "bd,dhc->bhc", condition_low, router_weight, preferred_element_type=jnp.float32
    ) + router_bias.astype(jnp.float32)
    sigmoid_out = jax.nn.sigmoid(logits)
    step_table = (
        timesteps[:, None] == jnp.arange(route_masks.shape[0], dtype=jnp.int32)[None, :]
    ).astype(jnp.float32)
    mask_rows = jnp.einsum(
        "bs,shc->bhc", step_table, route_masks.astype(jnp.float32), precision=HIGHEST
    )
    gate_values = mask_rows * sigmoid_out
    head_gate = gate_values[:, :, 0]
    group_gate = gate_values[:, :, 1]
    inputs_f = tokens.astype(jnp.float32).reshape(item_count, item_length, model_width)
    normed_one, inverse_one = layer_norm(inputs_f)
    hidden_one = (normed_one * (1.0 + scale_one) + shift_one).astype(jnp.bfloat16)
    projected = jnp.einsum(
        "bsd,dke->bske", hidden_one, input_weight, preferred_element_type=jnp.float32
    )
    input_bias_f = input_bias.astype(jnp.float32)
    head_shape = (item_count, item_length, local_heads, head_size)
    queries = (projected[:, :, 0] + input_bias_f[0]).astype(jnp.bfloat16).reshape(head_shape)
    keys_low = projected[:, :, 1].astype(jnp.bfloat16).reshape(head_shape)
    values_low = (projected[:, :, 2] + input_bias_f[1]).astype(jnp.bfloat16).reshape(head_shape)
    scores = (
        jnp.einsum("bqhe,bkhe->bhqk", queries, keys_low, preferred_element_type=jnp.float32)
        * score_scale
    )
    row_max = jnp.max(scores, axis=-1, keepdims=True)
    log_total = row_max + jnp.log(jnp.sum(jnp.exp(scores - row_max), axis=-1, keepdims=True))
    softmax_low = jnp.exp(scores - log_total).astype(jnp.bfloat16)
    mixed_heads = jnp.einsum(
        "bhqk,bkhe->bqhe", softmax_low, values_low, preferred_element_type=jnp.float32
    )
    gated_heads = (
        (mixed_heads * head_gate[:, None, :, None])
        .astype(jnp.bfloat16)
        .reshape(rows_all, local_width)
    )
    attention_part = jnp.dot(gated_heads, output_weight, preferred_element_type=jnp.float32)
    attention = (lax.psum(attention_part, "tensor") + output_bias.astype(jnp.float32)).reshape(
        item_count, item_length, model_width
    )
    residual_one = inputs_f + gate_one * attention
    normed_two, inverse_two = layer_norm(residual_one)
    hidden_two = (
        (normed_two * (1.0 + scale_two) + shift_two)
        .astype(jnp.bfloat16)
        .reshape(rows_all, model_width)
    )
    expanded = jnp.dot(
        hidden_two, expand_weight, preferred_element_type=jnp.float32
    ) + expand_bias.astype(jnp.float32)
    activated = gelu_tanh(expanded)
    group_shape = (item_count, item_length, local_heads, group_width)
    gated_channels = (
        (activated.reshape(group_shape) * group_gate[:, None, :, None])
        .astype(jnp.bfloat16)
        .reshape(rows_all, -1)
    )
    mlp_part = jnp.dot(gated_channels, reduce_weight, preferred_element_type=jnp.float32)
    branch_two = (lax.psum(mlp_part, "tensor") + reduce_bias.astype(jnp.float32)).reshape(
        item_count, item_length, model_width
    )
    block_output = residual_one + gate_two * branch_two
    cotangent = out_cotangent.astype(jnp.float32).reshape(item_count, item_length, model_width)
    gate_two_grad = jnp.sum(cotangent * branch_two, axis=1)
    branch_grad = (gate_two * cotangent).astype(jnp.bfloat16).reshape(rows_all, model_width)
    reduce_bias_grad = jnp.sum(branch_grad.astype(jnp.float32), axis=0)
    reduce_weight_grad = contract_rows(gated_channels, branch_grad)
    channel_blocks = contract_cols(branch_grad, reduce_weight).reshape(group_shape)
    group_gate_grad = jnp.sum(channel_blocks * activated.reshape(group_shape), axis=(1, 3))
    activated_grad = (channel_blocks * group_gate[:, None, :, None]).reshape(rows_all, -1)
    expanded_grad = jax.vjp(gelu_tanh, expanded)[1](activated_grad)[0].astype(jnp.bfloat16)
    expand_bias_grad = jnp.sum(expanded_grad.astype(jnp.float32), axis=0)
    expand_weight_grad = contract_rows(hidden_two, expanded_grad)
    hidden_two_part = contract_cols(expanded_grad, expand_weight)
    hidden_two_grad = lax.psum(hidden_two_part, "tensor").reshape(
        item_count, item_length, model_width
    )
    shift_two_grad = jnp.sum(hidden_two_grad, axis=1)
    scale_two_grad = jnp.sum(hidden_two_grad * normed_two, axis=1)
    residual_grad = cotangent + norm_back(
        hidden_two_grad * (1.0 + scale_two), normed_two, inverse_two
    )
    branch_one_grad = (gate_one * residual_grad).astype(jnp.bfloat16).reshape(rows_all, model_width)
    output_bias_grad = jnp.sum(branch_one_grad.astype(jnp.float32), axis=0)
    output_weight_grad = contract_rows(gated_heads, branch_one_grad)
    heads_grad = contract_cols(branch_one_grad, output_weight).reshape(head_shape)
    head_gate_grad = jnp.sum(heads_grad * mixed_heads, axis=(1, 3))
    mixed_grad = (heads_grad * head_gate[:, None, :, None]).astype(jnp.bfloat16)
    scores_again = (
        jnp.einsum("bqhe,bkhe->bhqk", queries, keys_low, preferred_element_type=jnp.float32)
        * score_scale
    )
    softmax_full = jnp.exp(scores_again - log_total)
    softmax_grad = jnp.einsum(
        "bqhe,bkhe->bhqk", mixed_grad, values_low, preferred_element_type=jnp.float32
    )
    values_grad = jnp.einsum(
        "bhqk,bqhe->bkhe",
        softmax_full.astype(jnp.bfloat16),
        mixed_grad,
        preferred_element_type=jnp.float32,
    )
    score_grad = (
        softmax_full * (softmax_grad - jnp.sum(softmax_grad * softmax_full, axis=-1, keepdims=True))
    ).astype(jnp.bfloat16)
    queries_grad = (
        jnp.einsum("bhqk,bkhe->bqhe", score_grad, keys_low, preferred_element_type=jnp.float32)
        * score_scale
    )
    keys_grad = (
        jnp.einsum("bhqk,bqhe->bkhe", score_grad, queries, preferred_element_type=jnp.float32)
        * score_scale
    )
    stacked_grad = (
        jnp.stack([queries_grad, keys_grad, values_grad], axis=2)
        .reshape(item_count, item_length, 3, local_width)
        .astype(jnp.bfloat16)
    )
    stacked_f = stacked_grad.astype(jnp.float32)
    input_bias_grad = jnp.stack(
        [jnp.sum(stacked_f[:, :, 0], axis=(0, 1)), jnp.sum(stacked_f[:, :, 2], axis=(0, 1))]
    )
    input_weight_grad = jnp.einsum(
        "bsd,bske->dke", hidden_one, stacked_grad, preferred_element_type=jnp.float32
    )
    hidden_one_part = jnp.einsum(
        "bske,dke->bsd", stacked_grad, input_weight, preferred_element_type=jnp.float32
    ).reshape(rows_all, model_width)
    hidden_one_grad = lax.psum(hidden_one_part, "tensor")
    gate_one_grad = jnp.sum(residual_grad * attention, axis=1)
    hidden_one_grad = hidden_one_grad.reshape(item_count, item_length, model_width)
    shift_one_grad = jnp.sum(hidden_one_grad, axis=1)
    scale_one_grad = jnp.sum(hidden_one_grad * normed_one, axis=1)
    tokens_grad = residual_grad + norm_back(
        hidden_one_grad * (1.0 + scale_one), normed_one, inverse_one
    )
    modulation_grad = jnp.stack(
        [
            shift_one_grad,
            scale_one_grad,
            gate_one_grad,
            shift_two_grad,
            scale_two_grad,
            gate_two_grad,
        ],
        axis=1,
    )
    column_start = lax.axis_index("tensor") * modulate_weight.shape[2]
    own_grad = lax.dynamic_slice_in_dim(modulation_grad, column_start, modulate_weight.shape[2], 2)
    modulate_weight_grad = jnp.einsum(
        "bd,bke->dke", silu_condition.astype(jnp.float32), own_grad, precision=HIGHEST
    )
    modulate_bias_grad = jnp.sum(own_grad, axis=0)
    gate_grad = jnp.stack([head_gate_grad, group_gate_grad], axis=-1)
    logit_grad = gate_grad * mask_rows * sigmoid_out * (1.0 - sigmoid_out)
    router_weight_grad = jnp.einsum(
        "bd,bhc->dhc", condition_low.astype(jnp.float32), logit_grad, precision=HIGHEST
    )
    router_bias_grad = jnp.sum(logit_grad, axis=0)
    summed = lax.psum(
        (
            modulate_weight_grad,
            modulate_bias_grad,
            input_weight_grad,
            input_bias_grad,
            output_weight_grad,
            output_bias_grad,
            expand_weight_grad,
            expand_bias_grad,
            reduce_weight_grad,
            reduce_bias_grad,
            router_weight_grad,
            router_bias_grad,
        ),
        "dp",
    )
    return (
        block_output.reshape(rows_all, model_width),
        tokens_grad.reshape(rows_all, model_width),
    ) + tuple(summed)


def solution(mesh):
    return jax.shard_map(
        body,
        mesh=mesh,
        in_specs=(
            P("dp", None),
            P("dp", None),
            P("dp"),
            P(None, "tensor", None),
            P(None, None, "tensor"),
            P(None, "tensor"),
            P(None, None, "tensor"),
            P(None, "tensor"),
            P("tensor", None),
            P(),
            P(None, "tensor"),
            P("tensor"),
            P("tensor", None),
            P(),
            P(None, "tensor", None),
            P("tensor", None),
            P("dp", None),
        ),
        out_specs=(
            P("dp", None),
            P("dp", None),
            P(None, None, "tensor"),
            P(None, "tensor"),
            P(None, None, "tensor"),
            P(None, "tensor"),
            P("tensor", None),
            P(),
            P(None, "tensor"),
            P("tensor"),
            P("tensor", None),
            P(),
            P(None, "tensor", None),
            P("tensor", None),
        ),
        check_vma=False,
    )
```

profile of v0, /device:TPU:0, one launch (start us, length us, event | category | flops | bytes accessed | tf_op | source)
XLA Modules:
  0.0 1134.2 jit_solution(17159783250025493048)
XLA Ops:
  15.8 29.1 %all_gather.3 = f32[8,6,1152]{1,0,2:T(8,128)} all-gather(f32[8,6,144]{1,0,2:T(8,128)S(1)} %copy.78), channel_id=1, replica_groups=mesh['dp'=4,'tensor'=8] {'tensor'}, dimensions={2}, use_global_device_ids=true | all-gather | bytes 248832 | tf_op jit(solution)/shard_map/all_gather | solution.py:72
  44.9 22.1 %fusion.64 = (f32[8,1,1152]{1,0,2:T(8,128)}, f32[8,1,1152]{1,0,2:T(8,128)}, f32[8,1,1152]{1,0,2:T(8,128)}, f32[8,1,1152]{1,0,2:T(8,128)}, f32[8,1,1152]{1,0,2:T(8,128)}, /*index=5*/f32[8,1,1152]{1,0,2:T(8,128)}) fusion(f32[8,6,1152]{1,0,2:T(8,128)} %all_gather.3), kind=kLoop, calls=%fused_computation.135 | loop fusion | bytes 442368 | tf_op jit(solution)/shard_map/slice | solution.py:74
  84.7 5.3 fusion.70
  113.9 5.1 broadcast_multiply_fusion
  126.1 102.3 %all-reduce.8.cloned.1.call-done = f32[2048,1152]{1,0:T(8,128)} async-done(((f32[2048,1152]{1,0:T(8,128)}), f32[2048,1152]{1,0:T(8,128)}) %all-reduce.8.cloned.1.call-update) | async-done | bytes 9437200 | tf_op jit(solution)/shard_map/psum | solution.py:116
  228.4 10.4 fusion.62
  238.8 4.9 multiply_reduce_fusion.4
  248.4 8.9 multiply_convert_fusion
  258.6 7.0 fusion.72
  265.7 9.8 fusion.71
  275.6 128.3 %all-reduce.10.cloned.1.call-done = f32[2048,1152]{1,0:T(8,128)} async-done(((f32[2048,1152]{1,0:T(8,128)}), f32[2048,1152]{1,0:T(8,128)}) %all-reduce.10.cloned.1.call-update) | async-done | bytes 9437200 | tf_op jit(solution)/shard_map/psum | solution.py:153
  403.8 8.1 fusion.9
  412.9 10.7 convert_reduce_fusion.1
  434.7 5.4 convolution_bitcast_fusion
  440.8 7.9 fusion.75
  457.8 6.6 fusion.22
  464.4 215.9 %all-reduce.12.cloned.1.call-done = (f32[2048,1152]{1,0:T(8,128)}, f32[2048,1152]{1,0:T(8,128)}) async-done(((f32[2048,1152]{1,0:T(8,128)}, f32[2048,1152]{1,0:T(8,128)}), (f32[2048,1152]{1,0:T(8,128)}, f32[2048,1152]{1,0:T(8,128)})) %all-reduce.12.cloned.1.call-update) | async-done | bytes 18874384 | tf_op jit(solution)/shard_map/psum | solution.py:137
  680.3 22.4 %fusion.7 = (f32[8,1152]{1,0:T(8,128)S(1)}, f32[8,1152]{1,0:T(8,128)S(1)}, f32[8,1152]{1,0:T(8,128)S(1)}, f32[8,1152]{1,0:T(8,128)S(1)}, f32[8,1152]{1,0:T(8,128...) fusion(f32[2048,1152]{1,0:T(8,128)} %all-reduce.10.cloned.1.call-done, f32[2048,1152]{1,0:T(8,128)} %all-reduce.8.cloned.1.call-done, ...), kind=kLoop, calls=%fused_computation.17 | loop fusion | flops 61286400 | bytes 56976384 | tf_op jit(solution)/shard_map/reduce_sum | solution.py:157
  711.2 5.8 fusion.21
  719.3 7.0 fusion.8
  726.3 11.0 fusion.2
  737.4 11.9 %multiply_add_fusion = f32[2048,1152]{1,0:T(8,128)} fusion(f32[2048,1152]{1,0:T(8,128)} %get-tuple-element.52, f32[2048,1152]{1,0:T(8,128)} %get-tuple-element.31, bf16[2048,1152]{1,0:T(8,128)(2,1)} %param.17, f32[2048]{0:T(1024)S(1)} %broadcast_multiply_fusion.1, f32[2048]{0:T(1024)S(1)} %broadcast_multiply_fusion.2, f32[2048]{0:T(1024)S(1)} %copy-done.30, ...), kind=kLoop, calls=%fused_computation.24 | loop fusion | flops 21233664 | bytes 33099776 | tf_op jit(solution)/shard_map/add | solution.py:212
  749.4 26.8 %all-reduce.1 = (f32[6,144]{1,0:T(8,128)}, f32[2,144]{1,0:T(2,128)}, f32[1152]{0:T(1024)}, f32[576]{0:T(1024)}, f32[1152]{0:T(1024)}, /*index=5*/f32[1152,2,2]{0,2,1:T(2,128)}, f32[2,2]{1,0:T(2,128)}) all-reduce(f32[6,144]{1,0:T(8,128)S(1)} %dynamic-slice_reduce_fusion, ...), channel_id=1, replica_groups=mesh['dp'=4,'tensor'=8] {'dp'}, use_global_device_ids=true, to_apply=%region_23.24 | all-reduce | flops 8644 | bytes 69152 | tf_op jit(solution)/shard_map/psum | solution.py:238
  776.2 341.5 %all-reduce.14.cloned.1.call-done = (f32[1152,6,144]{0,2,1:T(8,128)}, f32[1152,3,144]{0,2,1:T(8,128)}, f32[144,1152]{1,0:T(8,128)}, f32[1152,576]{0,1:T(8,128)}, f32[576,1152]{1,0:T(8,128)}) async-done(((f32[1152,6,144]{0,2,1:T(8,128)}, f32[1152,3,144]{0,2,1:T(8,128)}, f32[144,1152]{1,0:T(8,128)}, f32[1152,576]{0,1:T(8,128)}, f32[576,1152]{1,0:T(8,128)}), (f32[1152,6,144]{0,2,1:T(8,128)}, ...) | async-done | bytes 11943952 | tf_op jit(solution)/shard_map/psum | solution.py:238
  (219 shorter events, 105.1 us)
Async XLA Ops:
  7.2 7.6 copy-start
  7.2 7.0 copy-start.37
  7.2 7.6 copy-start.25
  7.2 221.2 %all-reduce.8.cloned.1.call-start = ((), (), s32[]{:S(2)}) async-start(), calls=%async_computation | async-start | bytes 18874368 | tf_op jit(solution)/shard_map/psum | solution.py:116
  10.4 34.5 %copy-start.27 = (f32[2048]{0:T(1024)}, f32[2048]{0:T(1024)S(1)}, u32[]{:S(2)}) copy-start(f32[2048]{0:T(1024)S(1)} %broadcast_multiply_fusion.6) | copy-start | bytes 24580
  90.0 313.8 %all-reduce.10.cloned.1.call-start = ((), (), s32[]{:S(2)}) async-start(), calls=%async_computation.1 | async-start | bytes 18874368 | tf_op jit(solution)/shard_map/psum | solution.py:153
  238.8 8.6 slice-start.2
  238.8 8.7 slice-start.4
  247.3 9.9 copy-start.13
  265.7 414.6 %all-reduce.12.cloned.1.call-start = ((), (), s32[]{:S(2)}) async-start(), calls=%async_computation.2 | async-start | bytes 37748736 | tf_op jit(solution)/shard_map/psum | solution.py:137
  403.8 9.1 copy-start.5
  412.9 10.7 copy-start.12
  440.1 8.6 slice-start
  440.1 677.6 %all-reduce.14.cloned.1.call-start = ((), (), s32[]{:S(2)}) async-start(), calls=%async_computation.3 | async-start | bytes 23887872 | tf_op jit(solution)/shard_map/psum | solution.py:238
  440.8 7.9 slice-start.1
  440.8 7.9 copy-start.54
  680.3 22.5 %copy-start.26 = (f32[8,1152]{1,0:T(8,128)S(1)}, f32[8,1152]{1,0:T(8,128)}, u32[]{:S(2)}) copy-start(f32[8,1152]{1,0:T(8,128)} %param.18) | copy-start | bytes 110596
  711.1 7.9 copy-start.43
  711.1 7.9 copy-start.44
  711.2 8.1 copy-start.28
  711.2 8.1 copy-start.30
  719.3 7.0 copy-start.24
  737.3 12.0 %copy-start.31 = (f32[1152]{0:T(1024)S(1)}, f32[1152]{0:T(1024)}, u32[]{:S(2)}) copy-start(f32[1152]{0:T(1024)} %get-tuple-element.46) | copy-start | bytes 13828
  737.3 12.0 %copy-start.40 = (f32[576]{0:T(1024)S(1)}, f32[576]{0:T(1024)}, u32[]{:S(2)}) copy-start(f32[576]{0:T(1024)} %get-tuple-element.58) | copy-start | bytes 6916
  (42 other events, 132.8 us)
Sparse Core Ops, SparseCore 0:
  90.1 138.1 all-reduce.7
  265.8 137.9 all-reduce.9
  440.2 240.0 all-reduce.11
  706.7 410.9 all-reduce.13
where the time goes:
time: 1140 us; the launch traced here: 1130 us
  waiting for transfers between devices  788 us (69%)
  other arithmetic  112 us (10%)
  matrix products  84.5 us (7%)
  local copies, waits for them, and re-layouts  78.5 us (7%)
  blocking collectives  55.9 us (5%)
  between operations  14.9 us (1%)
    psum x1, waiting for transfers between devices, body(): lax.psum((modulate_weight_grad, modulate_bias_grad, input_weight_grad, in...  341 us
    psum x1, waiting for transfers between devices, body(): lax.psum(mlp_part, 'tensor') + reduce_bias.astype(jnp.float32)  216 us
    psum x1, waiting for transfers between devices, body(): lax.psum(hidden_two_part, 'tensor')  128 us
    psum x1, waiting for transfers between devices, body(): lax.psum(attention_part, 'tensor') + output_bias.astype(jnp.float32)  102 us
    unnamed x144, local copies, waits for them, and re-layouts  51.7 us
    all_gather x1, blocking collectives, body(): modulation = lax.all_gather(modulate_part, 'tensor', axis=2, tiled=True)  29.1 us
    psum x1, blocking collectives, body(): lax.psum((modulate_weight_grad, modulate_bias_grad, input_weight_grad, in...  26.8 us
  transfers between devices with their start and end apart: 4, of which 4 were waited for; matrix products, arithmetic and copies ran while one was open for 10% of the time, Pallas kernels for 0%

commit v1 on v0

--- a/solution.py
+++ b/solution.py
@@ -150,9 +150,8 @@
     expand_bias_grad = jnp.sum(expanded_grad.astype(jnp.float32), axis=0)
     expand_weight_grad = contract_rows(hidden_two, expanded_grad)
     hidden_two_part = contract_cols(expanded_grad, expand_weight)
-    hidden_two_grad = lax.psum(hidden_two_part, "tensor").reshape(
-        item_count, item_length, model_width
-    )
+    target_clear = lambda inp: jnp.sum(lax.all_gather(inp, "tensor"), axis=0)
+    hidden_two_grad = target_clear(hidden_two_part).reshape(item_count, item_length, model_width)
     shift_two_grad = jnp.sum(hidden_two_grad, axis=1)
     scale_two_grad = jnp.sum(hidden_two_grad * normed_two, axis=1)
     residual_grad = cotangent + norm_back(

time: 1140 us -> 1370 us (1.20)
  waiting for transfers between devices: 788 us -> 987 us
  other arithmetic: 112 us -> 136 us
    all_gather x0 -> x1, waiting for transfers between devices: none -> 326 us  [body(): target_clear = lambda inp: jnp.sum(lax.all_gather(inp, 'tensor'), axis=0)]
    psum x1 -> x0, waiting for transfers between devices: 128 us -> none  [body(): lax.psum(hidden_two_part, 'tensor')]
    reduce_sum x0 -> x2, other arithmetic: none -> 35.4 us  [the longest x1 27.9 us: body(): target_clear = lambda inp: jnp.sum(lax.all_gather(inp, 'tensor'), axis=0)]
    unnamed x144 -> x159, local copies, waits for them, and re-layouts: 51.7 us -> 54.9 us
  transfers between devices with their start and end apart: 4 -> 4, of which waited for: 4 -> 4; matrix products, arithmetic and copies ran while one was open for 10% -> 8% of each run, Pallas kernels for 0% -> 0%
where the time goes in v1:
time: 1370 us; the launch traced here: 1360 us
  waiting for transfers between devices  987 us (72%)
  other arithmetic  136 us (10%)
  matrix products  86.9 us (6%)
  local copies, waits for them, and re-layouts  81.5 us (6%)
  blocking collectives  55.9 us (4%)
  between operations  15.2 us (1%)
    psum x1, waiting for transfers between devices, body(): lax.psum((modulate_weight_grad, modulate_bias_grad, input_weight_grad, in...  341 us
    all_gather x1, waiting for transfers between devices, body(): target_clear = lambda inp: jnp.sum(lax.all_gather(inp, 'tensor'), axis=0)  326 us
    psum x1, waiting for transfers between devices, body(): lax.psum(mlp_part, 'tensor') + reduce_bias.astype(jnp.float32)  216 us
    psum x1, waiting for transfers between devices, body(): lax.psum(attention_part, 'tensor') + output_bias.astype(jnp.float32)  103 us
    unnamed x159, local copies, waits for them, and re-layouts  54.9 us
    all_gather x1, blocking collectives, body(): modulation = lax.all_gather(modulate_part, 'tensor', axis=2, tiled=True)  29 us
    reduce_sum x1, other arithmetic, body(): target_clear = lambda inp: jnp.sum(lax.all_gather(inp, 'tensor'), axis=0)  27.9 us
  transfers between devices with their start and end apart: 4, of which 4 were waited for; matrix products, arithmetic and copies ran while one was open for 8% of the time, Pallas kernels for 0%

profile of v1, /device:TPU:0, one launch (start us, length us, event | category | flops | bytes accessed | tf_op | source)
XLA Modules:
  0.0 1362.4 jit_solution(10994043278582130933)
XLA Ops:
  13.6 29.0 %all_gather.9 = f32[8,6,1152]{1,0,2:T(8,128)} all-gather(f32[8,6,144]{1,0,2:T(8,128)S(1)} %copy.78), channel_id=1, replica_groups=mesh['dp'=4,'tensor'=8] {'tensor'}, dimensions={2}, use_global_device_ids=true | all-gather | bytes 248832 | tf_op jit(solution)/shard_map/all_gather | solution.py:72
  42.6 21.9 %fusion.64 = (f32[8,1,1152]{1,0,2:T(8,128)}, f32[8,1,1152]{1,0,2:T(8,128)}, f32[8,1,1152]{1,0,2:T(8,128)}, f32[8,1,1152]{1,0,2:T(8,128)}, f32[8,1,1152]{1,0,2:T(8,128)}, /*index=5*/f32[8,1,1152]{1,0,2:T(8,128)}) fusion(f32[8,6,1152]{1,0,2:T(8,128)} %all_gather.9), kind=kLoop, calls=%fused_computation.136 | loop fusion | bytes 442368 | tf_op jit(solution)/shard_map/slice | solution.py:74
  82.8 5.3 fusion.70
  106.5 4.9 broadcast_multiply_fusion
  123.3 103.2 %all-reduce.7.cloned.1.call-done = f32[2048,1152]{1,0:T(8,128)} async-done(((f32[2048,1152]{1,0:T(8,128)}), f32[2048,1152]{1,0:T(8,128)}) %all-reduce.7.cloned.1.call-update) | async-done | bytes 9437200 | tf_op jit(solution)/shard_map/psum | solution.py:116
  226.5 10.4 fusion.62
  246.5 9.3 multiply_convert_fusion
  257.2 6.6 fusion.72
  263.9 13.1 fusion.71
  277.0 326.3 %all-gather.3.cloned.1.call-done = f32[16384,1152]{1,0:T(8,128)} async-done(((f32[2048,1152]{1,0:T(8,128)}), f32[16384,1152]{1,0:T(8,128)}) %all-gather.3.cloned.1.call-update) | async-done | bytes 75497488 | tf_op jit(solution)/shard_map/all_gather | solution.py:153
  603.2 27.9 %reduce_sum.241 = f32[2048,1152]{1,0:T(8,128)} reduce(f32[8,2048,1152]{2,1,0:T(8,128)} %bitcast.28, f32[]{:T(128)} %constant.16.clone.1), dimensions={0}, to_apply=%region_8.9 | reduce | flops 16515072 | bytes 84934656 | tf_op jit(solution)/shard_map/reduce_sum | solution.py:153
  631.1 7.5 multiply_reduce_fusion.3
  643.1 8.6 convert_reduce_fusion.1
  662.7 5.4 convolution_bitcast_fusion
  668.8 7.9 fusion.75
  685.9 6.6 fusion.21
  692.4 215.7 %all-reduce.9.cloned.1.call-done = (f32[2048,1152]{1,0:T(8,128)}, f32[2048,1152]{1,0:T(8,128)}) async-done(((f32[2048,1152]{1,0:T(8,128)}, f32[2048,1152]{1,0:T(8,128)}), (f32[2048,1152]{1,0:T(8,128)}, f32[2048,1152]{1,0:T(8,128)})) %all-reduce.9.cloned.1.call-update) | async-done | bytes 18874384 | tf_op jit(solution)/shard_map/psum | solution.py:137
  908.2 22.5 %fusion.7 = (f32[8,1152]{1,0:T(8,128)S(1)}, f32[8,1152]{1,0:T(8,128)S(1)}, f32[8,1152]{1,0:T(8,128)S(1)}, f32[8,1152]{1,0:T(8,128)S(1)}, f32[8,1152]{1,0:T(8,128...) fusion(f32[2048,1152]{1,0:T(8,128)} %reduce_sum.241, f32[2048,1152]{1,0:T(8,128)} %all-reduce.7.cloned.1.call-done, ...), kind=kLoop, calls=%fused_computation.18 | loop fusion | flops 61286400 | bytes 56976384 | tf_op jit(solution)/shard_map/reduce_sum | solution.py:156
  939.2 5.8 fusion.20
  947.3 7.0 fusion.8
  954.3 11.0 fusion.2
  965.4 11.9 multiply_add_fusion
  977.4 26.9 %all-reduce.1 = (f32[6,144]{1,0:T(8,128)}, f32[2,144]{1,0:T(2,128)}, f32[1152]{0:T(1024)}, f32[576]{0:T(1024)}, f32[1152]{0:T(1024)}, /*index=5*/f32[1152,2,2]{0,2,1:T(2,128)}, f32[2,2]{1,0:T(2,128)}) all-reduce(f32[6,144]{1,0:T(8,128)S(1)} %dynamic-slice_reduce_fusion, ...), channel_id=1, replica_groups=mesh['dp'=4,'tensor'=8] {'dp'}, use_global_device_ids=true, to_apply=%region_23.24 | all-reduce | flops 8644 | bytes 69152 | tf_op jit(solution)/shard_map/psum | solution.py:237
  1004.3 341.5 %all-reduce.11.cloned.1.call-done = (f32[1152,6,144]{0,2,1:T(8,128)}, f32[1152,3,144]{0,2,1:T(8,128)}, f32[144,1152]{1,0:T(8,128)}, f32[1152,576]{0,1:T(8,128)}, f32[576,1152]{1,0:T(8,128)}) async-done(((f32[1152,6,144]{0,2,1:T(8,128)}, f32[1152,3,144]{0,2,1:T(8,128)}, f32[144,1152]{1,0:T(8,128)}, f32[1152,576]{0,1:T(8,128)}, f32[576,1152]{1,0:T(8,128)}), (f32[1152,6,144]{0,2,1:T(8,128)}, ...) | async-done | bytes 11943952 | tf_op jit(solution)/shard_map/psum | solution.py:237
  (236 shorter events, 111.0 us)
Async XLA Ops:
  7.2 219.3 %all-reduce.7.cloned.1.call-start = ((), (), s32[]{:S(2)}) async-start(), calls=%async_computation | async-start | bytes 18874368 | tf_op jit(solution)/shard_map/psum | solution.py:116
  11.1 31.5 %copy-start.30 = (f32[2048]{0:T(1024)}, f32[2048]{0:T(1024)S(1)}, u32[]{:S(2)}) copy-start(f32[2048]{0:T(1024)S(1)} %broadcast_multiply_fusion.6) | copy-start | bytes 24580
  12.6 58.8 %copy-start.37 = (f32[8,256]{1,0:T(8,128)}, f32[8,256]{1,0:T(8,128)S(1)}, u32[]{:S(2)}) copy-start(f32[8,256]{1,0:T(8,128)S(1)} %div.41) | copy-start | bytes 24580
  64.5 7.4 copy-start.52
  88.2 515.1 %all-gather.3.cloned.1.call-start = ((), (), s32[]{:S(2)}) async-start(), calls=%async_computation.1 | async-start | bytes 84934656 | tf_op jit(solution)/shard_map/all_gather | solution.py:153
  236.9 8.6 slice-start.5
  236.9 8.7 slice-start.7
  245.5 10.3 copy-start.14
  263.8 644.3 %all-reduce.9.cloned.1.call-start = ((), (), s32[]{:S(2)}) async-start(), calls=%async_computation.2 | async-start | bytes 37748736 | tf_op jit(solution)/shard_map/psum | solution.py:137
  631.1 9.1 copy-start.3
  631.1 10.3 slice-start
  631.1 11.5 slice-start.1
  643.1 8.6 copy-start.13
  668.1 8.6 slice-start.3
  668.1 677.6 %all-reduce.11.cloned.1.call-start = ((), (), s32[]{:S(2)}) async-start(), calls=%async_computation.3 | async-start | bytes 23887872 | tf_op jit(solution)/shard_map/psum | solution.py:237
  668.8 7.9 slice-start.4
  668.8 7.9 copy-start.58
  908.2 22.6 %copy-start.27 = (f32[8,1152]{1,0:T(8,128)S(1)}, f32[8,1152]{1,0:T(8,128)}, u32[]{:S(2)}) copy-start(f32[8,1152]{1,0:T(8,128)} %param.18) | copy-start | bytes 110596
  939.2 7.9 copy-start.47
  939.2 7.9 copy-start.48
  939.2 8.1 copy-start.31
  939.2 8.1 copy-start.33
  965.4 12.0 copy-start.36
  965.4 12.0 copy-start.44
  (49 other events, 170.7 us)
Sparse Core Ops, SparseCore 0:
  88.3 138.2 all-reduce.6
  263.9 339.2 all-gather.2
  668.2 239.8 all-reduce.8
  934.7 410.9 all-reduce.10
